TPU v7x, 512 devices: a whole 4x4x16 slice. The times are simulated.
512 devices in a mesh: replica: 64 (over z, y_hi, core), shard: 8 (over x, y_lo).
Axes of the slice: x: 4, y: 4 (y_hi: 2, y_lo: 2; y = y_hi * 2 + y_lo), z: 16, core: 2. Of those that a mesh axis runs over, the one named last changes fastest.
Arguments:
- frames_in: bfloat16 [512, 512, 768], P(('replica', 'shard')), may hold values from -6 to 6
- lengths: int32 [512], P(('replica', 'shard')), may hold values from 128 to 512, as said below
- up_weight: bfloat16 [768, 1536], P('shard'), may hold values from -0.21875 to 0.21875
- norm_gain: bfloat16 [768], P('shard'), may hold values from 0.25 to 1.75
- conv_kernel: bfloat16 [32, 768], P(None, 'shard'), may hold values from -1 to 1
- down_weight: bfloat16 [768, 768], P(None, 'shard'), may hold values from -0.21875 to 0.21875
- cotangent: bfloat16 [512, 512, 768], P(('replica', 'shard')), may hold values from -24 to 24
Outputs:
- result: bfloat16 [512, 512, 768], P(('replica', 'shard'))
- grad_in: bfloat16 [512, 512, 768], P(('replica', 'shard'))
- up_grad: float32 [768, 1536], P('shard')
- gain_grad: float32 [768], P('shard')
- kernel_grad: float32 [32, 768], P(None, 'shard')
- down_grad: float32 [768, 768], P(None, 'shard')
Inputs may be any that keep to these rules, and one draw needn't show every extreme that they name: `lengths`: each length is a multiple of 128; utterance 0 has 512 frames.
All inputs are finite; a program needn't handle non-finite values.
Results may differ from a plain program's by a relative error of at most 0.017.
Values may be sent and summed in bfloat16 or wider, within the bound.
A program may use at most 64 MiB of HBM per device.

v0:
```python
import jax
import jax.numpy as jnp
from jax import lax
from jax.sharding import PartitionSpec as P

EPS = 1e-05


def normalize(inputs):
    average = jnp.mean(inputs, axis=1, keepdims=True)
    centred = inputs - average
    inv_std = lax.rsqrt(jnp.mean(centred * centred, axis=1, keepdims=True) + EPS)
    return (centred * inv_std, inv_std)


def depthwise(signal, taps_f, front, back):
    frames = signal.shape[1]
    padded = jnp.pad(signal, ((0, 0), (front, back), (0, 0)))
    total = jnp.zeros_like(signal)
    for offset in range(taps_f.shape[0]):
        total = total + taps_f[offset] * padded[:, offset : offset + frames]
    return total


def tap_grads(grad, signal, front, back):
    frames = signal.shape[1]
    padded = jnp.pad(signal, ((0, 0), (front, back), (0, 0)))
    return jnp.stack(
        [
            jnp.sum(grad * padded[:, offset : offset + frames], axis=(0, 1))
            for offset in range(front + back + 1)
        ]
    )


def body(frames_in, lengths, up_weight, norm_gain, conv_kernel, down_weight, cotangent):
    utts, frames, width = frames_in.shape
    chans = up_weight.shape[1] // 2
    count_taps = conv_kernel.shape[0]
    front = count_taps // 2
    back = count_taps - 1 - front
    row_count = utts * frames
    live = (jnp.arange(frames, dtype=jnp.int32)[None, :] < lengths[:, None]).astype(jnp.float32)
    live_col = live.reshape(row_count, 1)
    inputs = frames_in.reshape(row_count, width).astype(jnp.float32)
    normed, inv_std = normalize(inputs)
    up_full, gain_bf, taps_bf = (
        lax.all_gather(up_weight, "shard", axis=0, tiled=True),
        lax.all_gather(norm_gain, "shard", axis=0, tiled=True),
        lax.all_gather(conv_kernel, "shard", axis=1, tiled=True),
    )
    gain_f = gain_bf.astype(jnp.float32)
    scaled = (normed * gain_f).astype(jnp.bfloat16)
    projected = jnp.dot(scaled, up_full, preferred_element_type=jnp.float32)
    values_half = projected[:, :chans]
    gate_sig = jax.nn.sigmoid(projected[:, chans:])
    gated = (values_half * gate_sig * live_col).astype(jnp.bfloat16)
    taps_f = taps_bf.astype(jnp.float32)
    gated_f = gated.astype(jnp.float32).reshape(utts, frames, chans)
    filtered = depthwise(gated_f, taps_f, front, back).reshape(row_count, chans)
    activated = (jax.nn.silu(filtered) * live_col).astype(jnp.bfloat16)
    upstream = cotangent.reshape(row_count, width)
    down_full = lax.all_gather(down_weight, "shard", axis=1, tiled=True)
    mixed = jnp.dot(activated, down_full, preferred_element_type=jnp.float32)
    d_act = lax.dot_general(
        upstream, down_full, (((1,), (1,)), ((), ())), preferred_element_type=jnp.float32
    )
    result = (inputs + mixed).astype(jnp.bfloat16)
    down_part = lax.dot_general(
        activated, upstream, (((0,), (0,)), ((), ())), preferred_element_type=jnp.float32
    )
    factor = 1.0 / float(utts * lax.axis_size("replica") * lax.axis_size("shard") * frames) ** 0.5
    filt_sig = jax.nn.sigmoid(filtered)
    d_filt = d_act * live_col * filt_sig * (1.0 + filtered * (1.0 - filt_sig))
    d_filt3 = d_filt.reshape(utts, frames, chans)
    kernel_part = tap_grads(d_filt3, gated_f, front, back)
    d_gated = depthwise(d_filt3, taps_f[::-1], back, front).reshape(row_count, chans) * live_col
    d_proj = jnp.concatenate(
        [d_gated * gate_sig, d_gated * values_half * gate_sig * (1.0 - gate_sig)], axis=1
    ).astype(jnp.bfloat16)
    up_part = lax.dot_general(
        scaled, d_proj, (((0,), (0,)), ((), ())), preferred_element_type=jnp.float32
    )
    d_scaled = lax.dot_general(
        d_proj, up_full, (((1,), (1,)), ((), ())), preferred_element_type=jnp.float32
    )
    gain_part = jnp.sum(d_scaled * normed, axis=0)
    d_normed = d_scaled * gain_f
    d_inputs = inv_std * (
        d_normed
        - jnp.mean(d_normed, axis=1, keepdims=True)
        - normed * jnp.mean(d_normed * normed, axis=1, keepdims=True)
    )
    grad_in = (upstream.astype(jnp.float32) + d_inputs).astype(jnp.bfloat16)
    slices = (
        lax.psum_scatter(
            up_part.astype(jnp.bfloat16), "shard", scatter_dimension=0, tiled=True
        ).astype(jnp.float32),
        lax.psum_scatter(
            gain_part.astype(jnp.bfloat16), "shard", scatter_dimension=0, tiled=True
        ).astype(jnp.float32),
        lax.psum_scatter(
            kernel_part.astype(jnp.bfloat16), "shard", scatter_dimension=1, tiled=True
        ).astype(jnp.float32),
        lax.psum_scatter(
            down_part.astype(jnp.bfloat16), "shard", scatter_dimension=1, tiled=True
        ).astype(jnp.float32),
    )
    up_total, gain_total, kernel_total, down_total = lax.psum(
        (slices[0], slices[1], slices[2], slices[3]), "replica"
    )
    return (
        result.reshape(utts, frames, width),
        grad_in.reshape(utts, frames, width),
        up_total * factor,
        gain_total * factor,
        kernel_total * factor,
        down_total * factor,
    )


def solution(mesh):
    return jax.shard_map(
        body,
        mesh=mesh,
        in_specs=(
            P(("replica", "shard"), None, None),
            P(("replica", "shard")),
            P("shard", None),
            P("shard"),
            P(None, "shard"),
            P(None, "shard"),
            P(("replica", "shard"), None, None),
        ),
        out_specs=(
            P(("replica", "shard"), None, None),
            P(("replica", "shard"), None, None),
            P("shard", None),
            P("shard"),
            P(None, "shard"),
            P(None, "shard"),
        ),
        check_vma=False,
    )
```

profile of v0, /device:TPU:6, one launch (start us, length us, event | category | flops | bytes accessed | tf_op | source)
XLA Modules:
  0.0 580.0 jit_solution(7954746644922215602)
XLA Ops:
  7.2 0.7 all-gather.4.cloned.1.call-update
  8.0 0.7 all-gather.6.cloned.1.call-update
  8.7 34.6 %all-gather = bf16[8,96,32]{1,2,0:T(8,128)(2,1)S(1)} all-gather(bf16[1,96,32]{1,2,0:T(8,128)(2,1)} %bitcast.209), channel_id=1, replica_groups=mesh['replica'=64,'shard'=8] {'shard'}, dimensions={0}, use_global_device_ids=true | all-gather | bytes 55296 | tf_op jit(solution)/shard_map/all_gather | solution.py:50
  45.0 0.6 fusion.79
  46.5 14.7 %all-reduce.2 = bf16[768]{0:T(1024)(128)(2,1)S(1)} all-reduce(bf16[768]{0:T(1024)(128)(2,1)S(1)} %dynamic-update-slice), channel_id=1, replica_groups=mesh['replica'=64,'shard'=8] {'shard'}, use_global_device_ids=true, to_apply=%add.2 | all-reduce | flops 768 | bytes 3072
  61.2 18.4 %all-gather.4.cloned.1.call-done = bf16[768,1536]{1,0:T(8,128)(2,1)} async-done(((bf16[96,1536]{1,0:T(8,128)(2,1)}), bf16[768,1536]{1,0:T(8,128)(2,1)}) %all-gather.4.cloned.1.call-update) | async-done | bytes 2359312 | tf_op jit(solution)/shard_map/all_gather | solution.py:48
  79.6 3.1 fusion.77
  83.2 1.2 copy-done
  84.4 0.9 copy-done.4
  85.3 7.4 %fusion.33 = f32[1,512,768]{2,1,0:T(8,128)} fusion(bf16[512,768]{1,0:T(8,128)(2,1)S(1)} %get-tuple-element.79, f32[768]{0:T(1024)S(1)} %get-tuple-element.41, f32[768]{0:T(1024)S(1)} %get-tuple-element.42, f32[768]{0:T(1024)S(1)} %get-tuple-element.43, f32[768]{0:T(1024)S(1)} %get-tuple-element.44, f32[768]{0:T(1024)S(1)} %get-tuple-element.45, ...), kind=kLoop, calls=%fused_computation.39 | loop fusion | flops 25165824 | bytes 4030464 | tf_op jit(solution)/shard_map/add | solution.py:21
  92.7 34.8 %all-gather.6.cloned.1.call-done = bf16[768,768]{0,1:T(8,128)(2,1)} async-done(((bf16[768,96]{0,1:T(8,128)(2,1)}), bf16[768,768]{0,1:T(8,128)(2,1)}) %all-gather.6.cloned.1.call-update) | async-done | bytes 1179664 | tf_op jit(solution)/shard_map/all_gather | solution.py:63
  127.5 5.7 multiply_reduce_fusion.1
  133.2 4.1 multiply_reduce_fusion
  138.2 0.8 copy.15
  139.1 3.2 convolution_convert_fusion.1
  142.6 9.2 %multiply_convert_fusion.2 = (bf16[512,768]{1,0:T(8,128)(2,1)S(1)}, f32[512,768]{1,0:T(8,128)S(1)}) fusion(f32[512,1536]{1,0:T(8,128)} %copy-done, f32[512]{0:T(512)S(1)} %fusion.71, f32[768]{0:T(1024)S(1)} %get-tuple-element.40, f32[768]{0:T(1024)S(1)} %get-tuple-element.59, f32[768]{0:T(1024)S(1)} %get-tuple-element.71, f32[768]{0:T(1024)S(1)} %get-tuple-element.70, ...), kind=kLoop, calls=%fused_computation.107 | loop fusion | flops 27131904 | bytes 7178240 | tf_op jit(solution)/shard_map/convert.64
  152.7 0.5 copy-done.10
  153.3 3.0 convolution_convert_fusion
  157.0 3.9 fusion.14
  160.8 16.3 %all-reduce.3 = bf16[768]{0:T(1024)(128)(2,1)S(1)} all-reduce(bf16[768]{0:T(1024)(128)(2,1)S(1)} %get-tuple-element.37), channel_id=3, replica_groups=mesh['replica'=64,'shard'=8] {'shard'}, use_global_device_ids=true, to_apply=%region_7.8.clone | all-reduce | flops 768 | bytes 3072
  177.2 1.5 fusion.64
  178.7 0.5 copy-done.12
  179.2 1.9 fusion.62
  181.2 1.5 reduce-scatter.10.cloned.1.call-done
  182.7 0.8 copy.16
  183.5 49.3 %reduce-scatter.8.cloned.1.call-done = bf16[768,96]{0,1:T(8,128)(2,1)} async-done(((bf16[768,768]{0,1:T(8,128)(2,1)}), bf16[768,96]{0,1:T(8,128)(2,1)}) %reduce-scatter.8.cloned.1.call-update) | async-done | bytes 147472 | tf_op jit(solution)/shard_map/reduce_scatter | solution.py:105
  232.8 68.0 %reduce-scatter.6.cloned.1.call-done = bf16[96,1536]{1,0:T(8,128)(2,1)} async-done(((bf16[768,1536]{1,0:T(8,128)(2,1)}), bf16[96,1536]{1,0:T(8,128)(2,1)}) %reduce-scatter.6.cloned.1.call-update) | async-done | bytes 294928 | tf_op jit(solution)/shard_map/reduce_scatter | solution.py:96
  300.8 269.9 %all-reduce.6 = (f32[96,1536]{1,0:T(8,128)S(1)}, f32[96]{0:T(128)S(1)}, f32[32,96]{1,0:T(8,128)S(1)}, f32[768,96]{0,1:T(8,128)S(1)}) all-reduce(bf16[96,1536]{1,0:T(8,128)(2,1)} %reduce-scatter.6.cloned.1.call-done, f32[96]{0:T(128)S(1)} %dynamic-slice_convert_fusion, ...), channel_id=1, replica_groups=mesh['replica'=64,'shard'=8] {'replica'}, use_global_device_ids=true, to_apply=%region_5.6 | all-reduce | flops 224352 | bytes 1346304 | tf_op jit(solution)/shard_map/psum | solution.py:109
  570.7 0.9 broadcast_multiply_fusion
  571.6 0.7 broadcast_multiply_fusion.1
  572.3 0.6 broadcast_multiply_fusion.2
  573.0 0.5 broadcast_multiply_fusion.6
  (82 shorter events, 3.7 us)
Async XLA Ops:
  7.2 37.9 %copy-start.11 = (u32[512]{0:T(512)S(1)}, u32[512]{0:T(512)}, u32[]{:S(2)}) copy-start(u32[512]{0:T(512)} %constant.30) | copy-start | bytes 6148
  7.2 36.6 %copy-start.2 = (bf16[1,512,768]{2,1,0:T(8,128)(2,1)S(1)}, bf16[1,512,768]{2,1,0:T(8,128)(2,1)}, u32[]{:S(2)}) copy-start(bf16[1,512,768]{2,1,0:T(8,128)(2,1)} %param.7) | copy-start | bytes 2359300
  7.2 39.1 %copy-start.13 = (bf16[96]{0:T(256)(128)(2,1)S(1)}, bf16[96]{0:T(256)(128)(2,1)}, u32[]{:S(2)}) copy-start(bf16[96]{0:T(256)(128)(2,1)} %param.10) | copy-start | bytes 580
  7.2 72.4 %all-gather.4.cloned.1.call-start = ((), (), s32[]{:S(2)}) async-start(), calls=%async_computation.3 | async-start | bytes 2654208 | tf_op jit(solution)/shard_map/all_gather | solution.py:48
  7.9 119.6 %all-gather.6.cloned.1.call-start = ((), (), s32[]{:S(2)}) async-start(), calls=%async_computation.4 | async-start | bytes 1327104 | tf_op jit(solution)/shard_map/all_gather | solution.py:63
  8.7 174.0 %reduce-scatter.10.cloned.1.call-start = ((), (), s32[]{:S(2)}) async-start(), calls=%async_computation.7 | async-start | bytes 221184
  82.8 1.7 copy-start
  84.4 0.9 copy-start.4
  133.2 4.1 copy-start.5
  137.3 1.8 copy-start.6
  139.0 93.7 %reduce-scatter.8.cloned.1.call-start = ((), (), s32[]{:S(2)}) async-start(), calls=%async_computation.6 | async-start | bytes 1327104 | tf_op jit(solution)/shard_map/reduce_scatter | solution.py:105
  142.3 158.5 %reduce-scatter.6.cloned.1.call-start = ((), (), s32[]{:S(2)}) async-start(), calls=%async_computation.5 | async-start | bytes 2654208 | tf_op jit(solution)/shard_map/reduce_scatter | solution.py:96
  142.6 9.2 %copy-start.1 = (f32[512,1536]{1,0:T(8,128)S(1)}, f32[512,1536]{1,0:T(8,128)}, u32[]{:S(2)}) copy-start(f32[512,1536]{1,0:T(8,128)} %copy-done) | copy-start | bytes 9437188
  151.8 0.9 copy-start.9
  151.8 1.4 copy-start.3
  152.3 0.9 copy-start.10
  156.9 20.3 %copy-start.8 = (bf16[1,512,768]{2,1,0:T(8,128)(2,1)S(1)}, bf16[1,512,768]{2,1,0:T(8,128)(2,1)}, u32[]{:S(2)}) copy-start(bf16[1,512,768]{2,1,0:T(8,128)(2,1)} %param.13) | copy-start | bytes 2359300
  177.2 1.5 copy-start.7
  177.2 2.0 copy-start.12
Sparse Core Ops, SparseCore 0:
  10.1 69.4 all-gather.3
  81.7 45.7 all-gather.5
  139.2 43.4 reduce-scatter.9
  185.6 47.1 reduce-scatter.7
  235.7 65.0 reduce-scatter.5
where the time goes:
time: 580 us
  blocking collectives  336 us (58%)
  waiting for transfers between devices  173 us (30%)
  other arithmetic  26.7 us (5%)
  matrix products  20.9 us (4%)
  between operations  16.2 us (3%)
  local copies, waits for them, and re-layouts  6.83 us (1%)
    psum x1, blocking collectives, body(): lax.psum((slices[0], slices[1], slices[2], slices[3]), 'replica')  270 us
    reduce_scatter x1, waiting for transfers between devices, body(): lax.psum_scatter(up_part.astype(jnp.bfloat16), 'shard', scatter_dimension...  68 us
    reduce_scatter x1, waiting for transfers between devices, body(): lax.psum_scatter(down_part.astype(jnp.bfloat16), 'shard', scatter_dimensi...  49.3 us
    all_gather x1, waiting for transfers between devices, body(): down_full = lax.all_gather(down_weight, 'shard', axis=1, tiled=True)  34.8 us
    all_gather x1, blocking collectives, body(): lax.all_gather(conv_kernel, 'shard', axis=1, tiled=True)  34.6 us
    unnamed x2, blocking collectives  31 us
    all_gather x1, waiting for transfers between devices, body(): lax.all_gather(up_weight, 'shard', axis=0, tiled=True)  18.4 us
  transfers between devices with their start and end apart: 5, of which 5 were waited for; matrix products, arithmetic and copies ran while one was open for 6% of the time, Pallas kernels for 0%

commit v1 on v0

--- a/solution.py
+++ b/solution.py
@@ -4,6 +4,11 @@
 from jax.sharding import PartitionSpec as P
 
 EPS = 1e-05
+
+
+def exchange_gather(x, axis, dim):
+    outgoing = jnp.stack([x] * lax.axis_size(axis))
+    return jnp.concatenate(lax.all_to_all(outgoing, axis, 0, 0), axis=dim)
 
 
 def normalize(inputs):
@@ -45,7 +50,7 @@
     inputs = frames_in.reshape(row_count, width).astype(jnp.float32)
     normed, inv_std = normalize(inputs)
     up_full, gain_bf, taps_bf = (
-        lax.all_gather(up_weight, "shard", axis=0, tiled=True),
+        exchange_gather(up_weight, "shard", 0),
         lax.all_gather(norm_gain, "shard", axis=0, tiled=True),
         lax.all_gather(conv_kernel, "shard", axis=1, tiled=True),
     )

time: 580 us -> 560 us (0.966)
  waiting for transfers between devices: 173 us -> 124 us
  blocking collectives: 336 us -> 350 us
  starting transfers between devices: 0.38 us -> 9.87 us
    all_gather x1, waiting for transfers between devices: 34.8 us -> 0.01 us  [body(): down_full = lax.all_gather(down_weight, 'shard', axis=1, tiled=True)]
    all_gather x1 -> x0, waiting for transfers between devices: 18.4 us -> none  [body(): lax.all_gather(up_weight, 'shard', axis=0, tiled=True)]
    all_gather x1, blocking collectives: 34.6 us -> 47.3 us  [body(): lax.all_gather(conv_kernel, 'shard', axis=1, tiled=True)]
    all_to_all x0 -> x1, starting transfers between devices: none -> 9.53 us  [exchange_gather(): return jnp.concatenate(lax.all_to_all(outgoing, axis, 0, 0), axis=dim)]
  transfers between devices with their start and end apart: 5 -> 5, of which waited for: 5 -> 3; matrix products, arithmetic and copies ran while one was open for 6% -> 7% of each run, Pallas kernels for 0% -> 0%
where the time goes in v1:
time: 560 us; the launch traced here: 559 us
  blocking collectives  350 us (62%)
  waiting for transfers between devices  124 us (22%)
  other arithmetic  28.5 us (5%)
  matrix products  19.5 us (3%)
  between operations  16.3 us (3%)
  local copies, waits for them, and re-layouts  11.2 us (2%)
  starting transfers between devices  9.87 us (2%)
    psum x1, blocking collectives, body(): lax.psum((slices[0], slices[1], slices[2], slices[3]), 'replica')  270 us
    reduce_scatter x1, waiting for transfers between devices, body(): lax.psum_scatter(up_part.astype(jnp.bfloat16), 'shard', scatter_dimension...  67.9 us
    reduce_scatter x1, waiting for transfers between devices, body(): lax.psum_scatter(down_part.astype(jnp.bfloat16), 'shard', scatter_dimensi...  49.4 us
    all_gather x1, blocking collectives, body(): lax.all_gather(conv_kernel, 'shard', axis=1, tiled=True)  47.3 us
    unnamed x2, blocking collectives  32.8 us
  transfers between devices with their start and end apart: 5, of which 3 were waited for; matrix products, arithmetic and copies ran while one was open for 7% of the time, Pallas kernels for 0%

profile of v1, /device:TPU:6, one launch (start us, length us, event | category | flops | bytes accessed | tf_op | source)
XLA Modules:
  0.0 559.1 jit_solution(2266948848682012421)
XLA Ops:
  7.2 2.6 stack.143
  9.7 9.5 %all-to-all-start = ((bf16[8,96,1536]{2,1,0:T(8,128)(2,1)}), bf16[8,96,1536]{2,1,0:T(8,128)(2,1)S(1)}, u32[]{:S(2)}, u32[]{:S(2)}) async-start(bf16[8,96,1536]{2,1,0:T(8,128)(2,1)} %stack.143), calls=%async_computation | async-start | bytes 4718592 | tf_op jit(solution)/shard_map/all_to_all | solution.py:11
  19.3 0.7 all-gather.3.cloned.1.call-update
  20.7 47.3 %all-gather = bf16[8,96,32]{1,2,0:T(8,128)(2,1)S(1)} all-gather(bf16[1,96,32]{1,2,0:T(8,128)(2,1)S(1)} %bitcast.214), channel_id=1, replica_groups=mesh['replica'=64,'shard'=8] {'shard'}, dimensions={0}, use_global_device_ids=true | all-gather | bytes 55296 | tf_op jit(solution)/shard_map/all_gather | solution.py:55
  69.0 0.6 fusion.89
  70.5 15.7 %all-reduce.2 = bf16[768]{0:T(1024)(128)(2,1)S(1)} all-reduce(bf16[768]{0:T(1024)(128)(2,1)S(1)} %dynamic-update-slice), channel_id=1, replica_groups=mesh['replica'=64,'shard'=8] {'shard'}, use_global_device_ids=true, to_apply=%add.2 | all-reduce | flops 768 | bytes 3072
  86.3 1.4 copy-done.6
  87.7 1.5 fusion.68
  89.7 1.2 copy-done
  90.9 0.9 copy-done.4
  91.8 7.4 %fusion.36 = f32[1,512,768]{2,1,0:T(8,128)} fusion(bf16[512,768]{1,0:T(8,128)(2,1)S(1)} %get-tuple-element.79, f32[768]{0:T(1024)S(1)} %get-tuple-element.41, f32[768]{0:T(1024)S(1)} %get-tuple-element.42, f32[768]{0:T(1024)S(1)} %get-tuple-element.43, f32[768]{0:T(1024)S(1)} %get-tuple-element.44, f32[768]{0:T(1024)S(1)} %get-tuple-element.45, ...), kind=kLoop, calls=%fused_computation.43 | loop fusion | flops 25165824 | bytes 4030464 | tf_op jit(solution)/shard_map/add | solution.py:26
  99.2 5.7 %multiply_reduce_fusion.1 = (bf16[768]{0:T(1024)(128)(2,1)S(1)}, bf16[768]{0:T(1024)(128)(2,1)S(1)}, bf16[768]{0:T(1024)(128)(2,1)S(1)}, bf16[768]{0:T(1024)(128...) fusion(f32[1,512,768]{2,1,0:T(8,128)S(1)} %get-tuple-element.78, ...), kind=kOutput, calls=%fused_computation.80 | convolution fusion | flops 617732352 | bytes 6706688 | tf_op jit(solution)/shard_map/dot_general | solution.py:70
  104.9 4.1 multiply_reduce_fusion
  109.9 0.8 copy.15
  110.8 3.2 convolution_convert_fusion.1
  114.3 9.2 %multiply_convert_fusion.2 = (bf16[512,768]{1,0:T(8,128)(2,1)S(1)}, f32[512,768]{1,0:T(8,128)S(1)}) fusion(f32[512,1536]{1,0:T(8,128)} %copy-done, f32[512]{0:T(512)S(1)} %fusion.84, f32[768]{0:T(1024)S(1)} %get-tuple-element.40, f32[768]{0:T(1024)S(1)} %get-tuple-element.59, f32[768]{0:T(1024)S(1)} %get-tuple-element.71, f32[768]{0:T(1024)S(1)} %get-tuple-element.70, ...), kind=kLoop, calls=%fused_computation.111 | loop fusion | flops 27131904 | bytes 7178240 | tf_op jit(solution)/shard_map/convert.64
  124.3 0.5 copy-done.11
  124.9 3.0 convolution_convert_fusion
  128.8 0.9 copy-done.7
  129.6 4.1 fusion.14
  133.7 17.1 %all-reduce.3 = bf16[768]{0:T(1024)(128)(2,1)S(1)} all-reduce(bf16[768]{0:T(1024)(128)(2,1)S(1)} %get-tuple-element.37), channel_id=3, replica_groups=mesh['replica'=64,'shard'=8] {'shard'}, use_global_device_ids=true, to_apply=%region_7.8.clone | all-reduce | flops 768 | bytes 3072
  150.9 3.3 fusion.71
  154.1 2.0 fusion.65
  156.1 6.1 %reduce-scatter.10.cloned.1.call-done = bf16[96,32]{1,0:T(8,128)(2,1)} async-done(((bf16[768,32]{1,0:T(8,128)(2,1)}), bf16[96,32]{1,0:T(8,128)(2,1)}) %reduce-scatter.10.cloned.1.call-update) | async-done | bytes 6160
  162.2 0.8 copy.16
  163.0 49.4 %reduce-scatter.8.cloned.1.call-done = bf16[768,96]{0,1:T(8,128)(2,1)} async-done(((bf16[768,768]{0,1:T(8,128)(2,1)}), bf16[768,96]{0,1:T(8,128)(2,1)}) %reduce-scatter.8.cloned.1.call-update) | async-done | bytes 147472 | tf_op jit(solution)/shard_map/reduce_scatter | solution.py:110
  212.4 67.9 %reduce-scatter.6.cloned.1.call-done = bf16[96,1536]{1,0:T(8,128)(2,1)} async-done(((bf16[768,1536]{1,0:T(8,128)(2,1)}), bf16[96,1536]{1,0:T(8,128)(2,1)}) %reduce-scatter.6.cloned.1.call-update) | async-done | bytes 294928 | tf_op jit(solution)/shard_map/reduce_scatter | solution.py:101
  280.3 269.5 %all-reduce.6 = (f32[96,1536]{1,0:T(8,128)S(1)}, f32[96]{0:T(128)S(1)}, f32[32,96]{1,0:T(8,128)S(1)}, f32[768,96]{0,1:T(8,128)S(1)}) all-reduce(bf16[96,1536]{1,0:T(8,128)(2,1)} %reduce-scatter.6.cloned.1.call-done, f32[96]{0:T(128)S(1)} %dynamic-slice_convert_fusion, ...), channel_id=1, replica_groups=mesh['replica'=64,'shard'=8] {'replica'}, use_global_device_ids=true, to_apply=%region_5.6 | all-reduce | flops 224352 | bytes 1346304 | tf_op jit(solution)/shard_map/psum | solution.py:114
  549.8 0.9 broadcast_multiply_fusion
  550.7 0.7 broadcast_multiply_fusion.1
  551.4 0.6 broadcast_multiply_fusion.2
  552.0 0.5 broadcast_multiply_fusion.6
  (86 shorter events, 3.7 us)
Async XLA Ops:
  9.7 11.0 %copy-start.12 = (bf16[32,96]{1,0:T(8,128)(2,1)S(1)}, bf16[32,96]{1,0:T(8,128)(2,1)}, u32[]{:S(2)}) copy-start(bf16[32,96]{1,0:T(8,128)(2,1)} %param.11) | copy-start | bytes 18436
  9.7 58.7 %copy-start.2 = (bf16[1,512,768]{2,1,0:T(8,128)(2,1)S(1)}, bf16[1,512,768]{2,1,0:T(8,128)(2,1)}, u32[]{:S(2)}) copy-start(bf16[1,512,768]{2,1,0:T(8,128)(2,1)} %param.7) | copy-start | bytes 2359300
  9.7 76.5 %all-to-all-start = ((bf16[8,96,1536]{2,1,0:T(8,128)(2,1)}), bf16[8,96,1536]{2,1,0:T(8,128)(2,1)S(1)}, u32[]{:S(2)}, u32[]{:S(2)}) async-start(bf16[8,96,1536]{2,1,0:T(8,128)(2,1)} %stack.143), calls=%async_computation | async-start | bytes 4718592 | tf_op jit(solution)/shard_map/all_to_all | solution.py:11
  19.3 49.7 %copy-start.13 = (u32[512]{0:T(512)S(1)}, u32[512]{0:T(512)}, u32[]{:S(2)}) copy-start(u32[512]{0:T(512)} %constant.30) | copy-start | bytes 6148
  19.3 51.0 %copy-start.15 = (bf16[96]{0:T(256)(128)(2,1)S(1)}, bf16[96]{0:T(256)(128)(2,1)}, u32[]{:S(2)}) copy-start(bf16[96]{0:T(256)(128)(2,1)} %param.10) | copy-start | bytes 580
  19.3 79.9 %all-gather.3.cloned.1.call-start = ((), (), s32[]{:S(2)}) async-start(), calls=%async_computation.4 | async-start | bytes 1327104 | tf_op jit(solution)/shard_map/all_gather | solution.py:68
  20.0 142.2 %reduce-scatter.10.cloned.1.call-start = ((), (), s32[]{:S(2)}) async-start(), calls=%async_computation.7 | async-start | bytes 221184
  86.3 1.4 copy-start.6
  89.2 1.7 copy-start
  90.9 0.9 copy-start.4
  104.9 4.1 copy-start.5
  109.0 1.8 copy-start.8
  110.7 101.7 %reduce-scatter.8.cloned.1.call-start = ((), (), s32[]{:S(2)}) async-start(), calls=%async_computation.6 | async-start | bytes 1327104 | tf_op jit(solution)/shard_map/reduce_scatter | solution.py:110
  114.0 166.3 %reduce-scatter.6.cloned.1.call-start = ((), (), s32[]{:S(2)}) async-start(), calls=%async_computation.5 | async-start | bytes 2654208 | tf_op jit(solution)/shard_map/reduce_scatter | solution.py:101
  114.2 9.2 %copy-start.1 = (f32[512,1536]{1,0:T(8,128)S(1)}, f32[512,1536]{1,0:T(8,128)}, u32[]{:S(2)}) copy-start(f32[512,1536]{1,0:T(8,128)} %copy-done) | copy-start | bytes 9437188
  123.5 0.9 copy-start.10
  123.5 1.4 copy-start.3
  124.0 0.9 copy-start.11
  127.9 1.7 copy-start.7
  150.9 3.3 copy-start.9
  150.9 3.3 copy-start.14
Sparse Core Ops, SparseCore 0:
  22.2 47.6 all-gather.2
  110.8 51.3 reduce-scatter.9
  165.3 47.0 reduce-scatter.7
  215.4 64.8 reduce-scatter.5
